TPU v7x, 32 devices: a whole 2x2x4 slice. The times are simulated.
32 devices in a mesh: rep: 2 (over y), span: 2 (over x), seq: 4 (over z), head: 2 (over core).
Axes of the slice: x: 2, y: 2, z: 4, core: 2. Of those that a mesh axis runs over, the one named last changes fastest.
Arguments:
- queries: bfloat16 [4, 2, 1024, 4096], P(('rep', 'span'), 'head', None, 'seq'), parts along dimension 0, may hold values from -12 to 12
- keys: bfloat16 [4, 2, 1024, 4096], P(('rep', 'span'), 'head', None, 'seq'), parts along dimension 0, may hold values from -12 to 12
- values: bfloat16 [4, 2, 1024, 4096], P(('rep', 'span'), 'head', None, 'seq'), parts along dimension 0, may hold values from -6 to 6
- span_order: int32 [4], P('rep'), parts along dimension 0, may hold values from 0 to 15, as said below
Outputs:
- attention: bfloat16 [4, 2, 1024, 4096], P(('rep', 'span'), 'head', 'seq'), parts along dimension 0
There are 2 independent parts, one for each index of `rep`. A program takes and returns all parts, laid end to end along the dimension named above; each array names one. Nothing has to cross between parts.
Inputs may be any that keep to these rules, and one draw needn't show every extreme that they name: `span_order`: each group has a different span index.
All inputs are finite; a program needn't handle non-finite values.
Results may differ from a plain program's by a relative error of at most 0.0055.
Values may be sent and summed in bfloat16 or wider, within the bound.
A program may use at most 128 MiB of HBM per device.

v0:
```python
import math
import jax
import jax.numpy as jnp
from jax import lax
from jax.sharding import PartitionSpec as P

HD = 128


def lookup(span_order, block_index):
    table = jnp.arange(span_order.shape[0], dtype=jnp.int32)
    return jnp.sum(
        jnp.where(block_index[:, None] == table[None, :], span_order[None, :], 0), axis=1
    )


def initial(query_heads):
    query_count = query_heads.shape[0]
    local_heads = query_heads.shape[1]
    return (
        jnp.full((local_heads, query_count), -1e30, jnp.float32),
        jnp.zeros((local_heads, query_count), jnp.float32),
        jnp.zeros((local_heads, query_count, HD), jnp.float32),
    )


def attend(running, query_heads, key_piece, value_piece, block_span, own_span, bias_rate):
    block_count = key_piece.shape[0]
    piece_rows = key_piece.shape[1]
    local_heads = key_piece.shape[2] // HD
    key_count = block_count * piece_rows
    score_scale = 1.0 / math.sqrt(HD)
    key_spans = jnp.repeat(block_span, piece_rows)
    allowed = key_spans <= own_span
    distance_bias = (own_span - key_spans).astype(jnp.float32) * jnp.float32(bias_rate)
    block_size = 1024
    block_total = key_count // block_size
    key_blocks = key_piece.reshape(block_total, block_size, local_heads, HD)
    value_blocks = value_piece.reshape(block_total, block_size, local_heads, HD)
    allow_blocks = allowed.reshape(block_total, block_size)
    bias_blocks = distance_bias.reshape(block_total, block_size)

    def advance(status, block_item):
        key_block, value_block, allow_block, bias_block = block_item
        maxima, totals, weighted = status
        scores = (
            jnp.einsum("qhd,khd->hqk", query_heads, key_block, preferred_element_type=jnp.float32)
            * score_scale
        )
        scores = scores - bias_block[None, None, :]
        scores = jnp.where(allow_block[None, None, :], scores, jnp.float32(-1e30))
        new_max = jnp.maximum(maxima, jnp.max(scores, axis=2))
        weights = jnp.where(
            allow_block[None, None, :], jnp.exp(scores - new_max[:, :, None]), 0.0
        ).astype(jnp.bfloat16)
        shrink = jnp.exp(maxima - new_max)
        totals = totals * shrink + jnp.sum(weights.astype(jnp.float32), axis=2)
        weighted = weighted * shrink[:, :, None] + jnp.einsum(
            "hqk,khd->hqd", weights, value_block, preferred_element_type=jnp.float32
        )
        return ((new_max, totals, weighted), None)

    running, unused = lax.scan(
        advance, running, (key_blocks, value_blocks, allow_blocks, bias_blocks)
    )
    return running


def finish(running):
    maxima, totals, weighted = running
    local_heads = weighted.shape[0]
    query_count = weighted.shape[1]
    output = (weighted / totals[:, :, None]).transpose(1, 0, 2)
    return output.reshape(1, 1, query_count, local_heads * HD).astype(jnp.bfloat16)


def per_device(queries, keys, values, span_order):
    half_rows = queries.shape[2]
    local_width = queries.shape[3]
    local_heads = local_width // HD
    halves = lax.axis_size("head")
    bias_rate = 1.0 / (2.0 * span_order.shape[0])
    own_span = lookup(span_order, jnp.reshape(lax.axis_index("span"), (1,)))[0]
    query_heads = queries.reshape(half_rows, local_heads, HD)
    pieces = (
        lax.all_gather(keys, ("span", "head"), axis=0, tiled=True),
        lax.all_gather(values, ("span", "head"), axis=0, tiled=True),
    )
    count = pieces[0].shape[0]
    block_index = jnp.arange(count, dtype=jnp.int32) // halves
    key_piece = pieces[0].reshape(count, half_rows, local_width)
    value_piece = pieces[1].reshape(count, half_rows, local_width)
    running = attend(
        initial(query_heads),
        query_heads,
        key_piece,
        value_piece,
        lookup(span_order, block_index),
        own_span,
        bias_rate,
    )
    result = finish(running)
    return lax.all_to_all(result, "seq", split_axis=2, concat_axis=3, tiled=True)


def solution(mesh):
    return jax.shard_map(
        per_device,
        mesh=mesh,
        in_specs=(
            P(("rep", "span"), "head", None, "seq"),
            P(("rep", "span"), "head", None, "seq"),
            P(("rep", "span"), "head", None, "seq"),
            P("rep"),
        ),
        out_specs=P(("rep", "span"), "head", "seq", None),
        check_vma=False,
    )
```

profile of v0, /device:TPU:0, one launch (start us, length us, event | category | flops | bytes accessed | tf_op | source)
XLA Modules:
  0.0 445.6 jit_solution(3276279276303057130)
XLA Ops:
  15.2 54.7 %all-gather.3.cloned.1.call-done = bf16[4,1,1024,1024]{3,2,1,0:T(8,128)(2,1)} async-done(((bf16[1,1,1024,1024]{3,2,1,0:T(8,128)(2,1)}), bf16[4,1,1024,1024]{3,2,1,0:T(8,128)(2,1)}) %all-gather.3.cloned.1.call-update) | async-done | bytes 8388624 | tf_op jit(solution)/shard_map/all_gather | solution.py:86
  69.9 11.6 %copy.38 = bf16[4,1,1024,1024]{2,3,0,1:T(8,128)(2,1)} copy(bf16[4,1,1024,1024]{3,2,1,0:T(8,128)(2,1)} %all-gather.3.cloned.1.call-done) | data formatting | bytes 16777216 | tf_op jit(solution)/shard_map/all_gather | solution.py:86
  81.5 48.2 %all-gather.5.cloned.1.call-done = bf16[4,1,1024,1024]{3,2,1,0:T(8,128)(2,1)} async-done(((bf16[1,1,1024,1024]{3,2,1,0:T(8,128)(2,1)}), bf16[4,1,1024,1024]{3,2,1,0:T(8,128)(2,1)}) %all-gather.5.cloned.1.call-update) | async-done | bytes 8388624 | tf_op jit(solution)/shard_map/all_gather | solution.py:87
  129.8 11.4 %copy.40 = bf16[4,1,1024,1024]{2,3,0,1:T(8,128)(2,1)} copy(bf16[4,1,1024,1024]{3,2,1,0:T(8,128)(2,1)} %all-gather.5.cloned.1.call-done) | data formatting | bytes 16777216 | tf_op jit(solution)/shard_map/all_gather | solution.py:87
  141.3 199.1 %while.15 = (s32[]{:T(128)}, f32[8,1024]{1,0:T(8,128)S(1)}, f32[8,1024]{1,0:T(8,128)S(1)}, f32[8,1024,128]{2,1,0:T(8,128)}, pred[4,1024]{1,0:T(4,128)(4,1)S(1)},...) while((s32[]{:T(128)}, f32[8,1024]{1,0:T(8,128)S(1)}, ...), condition=%wide.region_5.6_spmd.clone, body=%wide.region_2.5_spmd.clone.sunk | while | flops 4398817280 | bytes 115856512 | solution.py:63
  141.3 16.6 %bitcast_reduce_fusion.2 = (f32[8,1024]{1,0:T(8,128)S(1)}, f32[8,1024,1024]{2,1,0:T(8,128)}) fusion(f32[1024]{0:T(1024)S(1)} %bitcast.57, pred[1024]{0:T(1024)(128)(4,1)S(1)} %dynamic-slice_reduce_fusion.2, bf16[1024,8,128]{2,0,1:T(8,128)(2,1)S(1)} %get-tuple-element.240, bf16[4,1024,8,128]{1,3,2,0:T(8,128)(2,1)} %get-tuple-element.239, ...), kind=kOutput, calls=%fused_computation.1.clone.1 | convolution fusion | flops 2181029888 | bytes 37787136 | tf_op jit(solution)/shard_map/while/body/eval_jaxpr/qhd,khd->hqk/dot_general | solution.py:47
  157.9 21.6 %convert_reduce_fusion.2 = (f32[8,1024]{1,0:T(8,128)S(1)}, bf16[8,1024,1024]{1,2,0:T(8,128)(2,1)}) fusion(f32[8,1024]{1,0:T(8,128)S(1)} %select_maximum_fusion.2, f32[1024]{0:T(1024)S(1)} %bitcast.58, f32[8,1024,1024]{2,1,0:T(8,128)} %get-tuple-element.207, pred[1024]{0:T(1024)(128)(4,1)S(1)} %dynamic-slice_reduce_fusion.2), kind=kLoop, calls=%fused_computation.5.clone.1 | loop fusion | flops 67100672 | bytes 50402304 | tf_op jit(solution)/shard_map/while/body/eval_jaxpr/reduce_sum | solution.py:57
  179.5 11.0 %fusion.29 = f32[8,1024,128]{2,1,0:T(8,128)} fusion(f32[8,1024,128]{2,1,0:T(8,128)} %get-tuple-element.226, f32[8,1024]{1,0:T(8,128)S(1)} %get-tuple-element.210, pred[]{:T(512)S(6)} %compare.7, bf16[8,1024,1024]{1,2,0:T(8,128)(2,1)} %get-tuple-element.211, bf16[4,1024,8,128]{1,3,2,0:T(8,128)(2,1)} %get-tuple-element.242, s32[]{:T(128)} %get-tuple-element.223), kind=kOutput, calls=%fused_computation.8.clone.1 | convolution fusion | flops 2150629376 | bytes 27296256 | tf_op jit(solution)/shard_map/while/body/eval_jaxpr/hqk,khd->hqd/dot_general | solution.py:58
  190.5 16.6 %bitcast_reduce_fusion.2 = (f32[8,1024]{1,0:T(8,128)S(1)}, f32[8,1024,1024]{2,1,0:T(8,128)}) fusion(f32[1024]{0:T(1024)S(1)} %bitcast.57, pred[1024]{0:T(1024)(128)(4,1)S(1)} %dynamic-slice_reduce_fusion.2, bf16[1024,8,128]{2,0,1:T(8,128)(2,1)S(1)} %get-tuple-element.240, bf16[4,1024,8,128]{1,3,2,0:T(8,128)(2,1)} %get-tuple-element.239, ...), kind=kOutput, calls=%fused_computation.1.clone.1 | convolution fusion | flops 2181029888 | bytes 37787136 | tf_op jit(solution)/shard_map/while/body/eval_jaxpr/qhd,khd->hqk/dot_general | solution.py:47
  207.1 21.6 %convert_reduce_fusion.2 = (f32[8,1024]{1,0:T(8,128)S(1)}, bf16[8,1024,1024]{1,2,0:T(8,128)(2,1)}) fusion(f32[8,1024]{1,0:T(8,128)S(1)} %select_maximum_fusion.2, f32[1024]{0:T(1024)S(1)} %bitcast.58, f32[8,1024,1024]{2,1,0:T(8,128)} %get-tuple-element.207, pred[1024]{0:T(1024)(128)(4,1)S(1)} %dynamic-slice_reduce_fusion.2), kind=kLoop, calls=%fused_computation.5.clone.1 | loop fusion | flops 67100672 | bytes 50402304 | tf_op jit(solution)/shard_map/while/body/eval_jaxpr/reduce_sum | solution.py:57
  228.7 11.7 %fusion.29 = f32[8,1024,128]{2,1,0:T(8,128)} fusion(f32[8,1024,128]{2,1,0:T(8,128)} %get-tuple-element.226, f32[8,1024]{1,0:T(8,128)S(1)} %get-tuple-element.210, pred[]{:T(512)S(6)} %compare.7, bf16[8,1024,1024]{1,2,0:T(8,128)(2,1)} %get-tuple-element.211, bf16[4,1024,8,128]{1,3,2,0:T(8,128)(2,1)} %get-tuple-element.242, s32[]{:T(128)} %get-tuple-element.223), kind=kOutput, calls=%fused_computation.8.clone.1 | convolution fusion | flops 2150629376 | bytes 27296256 | tf_op jit(solution)/shard_map/while/body/eval_jaxpr/hqk,khd->hqd/dot_general | solution.py:58
  240.5 16.6 %bitcast_reduce_fusion.2 = (f32[8,1024]{1,0:T(8,128)S(1)}, f32[8,1024,1024]{2,1,0:T(8,128)}) fusion(f32[1024]{0:T(1024)S(1)} %bitcast.57, pred[1024]{0:T(1024)(128)(4,1)S(1)} %dynamic-slice_reduce_fusion.2, bf16[1024,8,128]{2,0,1:T(8,128)(2,1)S(1)} %get-tuple-element.240, bf16[4,1024,8,128]{1,3,2,0:T(8,128)(2,1)} %get-tuple-element.239, ...), kind=kOutput, calls=%fused_computation.1.clone.1 | convolution fusion | flops 2181029888 | bytes 37787136 | tf_op jit(solution)/shard_map/while/body/eval_jaxpr/qhd,khd->hqk/dot_general | solution.py:47
  257.1 21.6 %convert_reduce_fusion.2 = (f32[8,1024]{1,0:T(8,128)S(1)}, bf16[8,1024,1024]{1,2,0:T(8,128)(2,1)}) fusion(f32[8,1024]{1,0:T(8,128)S(1)} %select_maximum_fusion.2, f32[1024]{0:T(1024)S(1)} %bitcast.58, f32[8,1024,1024]{2,1,0:T(8,128)} %get-tuple-element.207, pred[1024]{0:T(1024)(128)(4,1)S(1)} %dynamic-slice_reduce_fusion.2), kind=kLoop, calls=%fused_computation.5.clone.1 | loop fusion | flops 67100672 | bytes 50402304 | tf_op jit(solution)/shard_map/while/body/eval_jaxpr/reduce_sum | solution.py:57
  278.7 11.7 %fusion.29 = f32[8,1024,128]{2,1,0:T(8,128)} fusion(f32[8,1024,128]{2,1,0:T(8,128)} %get-tuple-element.226, f32[8,1024]{1,0:T(8,128)S(1)} %get-tuple-element.210, pred[]{:T(512)S(6)} %compare.7, bf16[8,1024,1024]{1,2,0:T(8,128)(2,1)} %get-tuple-element.211, bf16[4,1024,8,128]{1,3,2,0:T(8,128)(2,1)} %get-tuple-element.242, s32[]{:T(128)} %get-tuple-element.223), kind=kOutput, calls=%fused_computation.8.clone.1 | convolution fusion | flops 2150629376 | bytes 27296256 | tf_op jit(solution)/shard_map/while/body/eval_jaxpr/hqk,khd->hqd/dot_general | solution.py:58
  290.5 16.6 %bitcast_reduce_fusion.2 = (f32[8,1024]{1,0:T(8,128)S(1)}, f32[8,1024,1024]{2,1,0:T(8,128)}) fusion(f32[1024]{0:T(1024)S(1)} %bitcast.57, pred[1024]{0:T(1024)(128)(4,1)S(1)} %dynamic-slice_reduce_fusion.2, bf16[1024,8,128]{2,0,1:T(8,128)(2,1)S(1)} %get-tuple-element.240, bf16[4,1024,8,128]{1,3,2,0:T(8,128)(2,1)} %get-tuple-element.239, ...), kind=kOutput, calls=%fused_computation.1.clone.1 | convolution fusion | flops 2181029888 | bytes 37787136 | tf_op jit(solution)/shard_map/while/body/eval_jaxpr/qhd,khd->hqk/dot_general | solution.py:47
  307.0 21.6 %convert_reduce_fusion.2 = (f32[8,1024]{1,0:T(8,128)S(1)}, bf16[8,1024,1024]{1,2,0:T(8,128)(2,1)}) fusion(f32[8,1024]{1,0:T(8,128)S(1)} %select_maximum_fusion.2, f32[1024]{0:T(1024)S(1)} %bitcast.58, f32[8,1024,1024]{2,1,0:T(8,128)} %get-tuple-element.207, pred[1024]{0:T(1024)(128)(4,1)S(1)} %dynamic-slice_reduce_fusion.2), kind=kLoop, calls=%fused_computation.5.clone.1 | loop fusion | flops 67100672 | bytes 50402304 | tf_op jit(solution)/shard_map/while/body/eval_jaxpr/reduce_sum | solution.py:57
  328.7 11.7 %fusion.29 = f32[8,1024,128]{2,1,0:T(8,128)} fusion(f32[8,1024,128]{2,1,0:T(8,128)} %get-tuple-element.226, f32[8,1024]{1,0:T(8,128)S(1)} %get-tuple-element.210, pred[]{:T(512)S(6)} %compare.7, bf16[8,1024,1024]{1,2,0:T(8,128)(2,1)} %get-tuple-element.211, bf16[4,1024,8,128]{1,3,2,0:T(8,128)(2,1)} %get-tuple-element.242, s32[]{:T(128)} %get-tuple-element.223), kind=kOutput, calls=%fused_computation.8.clone.1 | convolution fusion | flops 2150629376 | bytes 27296256 | tf_op jit(solution)/shard_map/while/body/eval_jaxpr/hqk,khd->hqd/dot_general | solution.py:58
  340.4 5.4 %copy.44 = f32[8,1024,128]{1,2,0:T(8,128)} copy(f32[8,1024,128]{2,1,0:T(8,128)} %get-tuple-element.53) | data formatting | bytes 8388608 | tf_op jit(solution)/shard_map/while | solution.py:63
  348.6 7.7 %copy.45 = bf16[1,1,1024,1024]{3,1,0,2:T(2,128)(2,1)} copy(bf16[1,1,1024,1024]{2,3,1,0:T(8,128)(2,1)S(1)} %bitcast.51) | data formatting | bytes 4194304 | tf_op jit(solution)/shard_map/convert_element_type | solution.py:74
  356.8 13.0 %reduce.4 = bf16[1024,1024]{1,0:T(8,128)(2,1)S(1)} reduce(bf16[1024,1,1,1024]{3,2,1,0:T(2,128)(2,1)} %bitcast.49, bf16[]{:T(256)} %broadcast.88), dimensions={1,2}, to_apply=%bitcast.30.reduce_sub_computation | reduce | bytes 4194306
  372.6 53.2 %all_to_all.18 = bf16[4,2,131072]{2,1,0:T(2,128)(2,1)S(1)} all-to-all(bf16[4,2,131072]{2,1,0:T(2,128)(2,1)} %reshape.51), channel_id=1, replica_groups=mesh['rep'=2,'span'=2,'seq'=4,'head'=2] {'seq'}, dimensions={0} | all-to-all | bytes 4194304 | tf_op jit(solution)/shard_map/all_to_all | solution.py:103
  425.8 3.4 reshape.52
  429.1 3.0 copy.51
  434.7 4.1 copy.47
  (44 shorter events, 17.6 us)
Async XLA Ops:
  6.5 63.4 %all-gather.3.cloned.1.call-start = ((), (), s32[]{:S(2)}) async-start(), calls=%async_computation.1 | async-start | bytes 10485760 | tf_op jit(solution)/shard_map/all_gather | solution.py:86
  7.3 122.5 %all-gather.5.cloned.1.call-start = ((), (), s32[]{:S(2)}) async-start(), calls=%async_computation.2 | async-start | bytes 10485760 | tf_op jit(solution)/shard_map/all_gather | solution.py:87
  8.0 5.3 %copy-start.1 = (s32[2]{0:T(128)S(1)}, s32[2]{0:T(128)}, u32[]{:S(2)}) copy-start(s32[2]{0:T(128)} %param.9) | copy-start | bytes 28
  81.5 59.7 %copy-start = (bf16[1024,8,128]{2,0,1:T(8,128)(2,1)S(1)}, bf16[1024,8,128]{2,0,1:T(8,128)(2,1)}, u32[]{:S(2)}) copy-start(bf16[1024,8,128]{2,0,1:T(8,128)(2,1)} %copy.42) | copy-start | bytes 6291460
Sparse Core Ops, SparseCore 0:
  8.9 60.9 all-gather.2
  71.5 58.2 all-gather.4
where the time goes:
time: 447 us; the launch traced here: 446 us
  matrix products  112 us (25%)
  waiting for transfers between devices  104 us (23%)
  other arithmetic  104 us (23%)
  local copies, waits for them, and re-layouts  57.9 us (13%)
  blocking collectives  53.2 us (12%)
  between operations  13.5 us (3%)
    reduce_sum x4, other arithmetic, advance(): totals = totals * shrink + jnp.sum(weights.astype(jnp.float32), axis=2)  86.4 us
    dot_general x4, matrix products, advance(): jnp.einsum('qhd,khd->hqk', query_heads, key_block, preferred_element_type...  66.3 us
    all_gather x1, waiting for transfers between devices, per_device(): lax.all_gather(keys, ('span', 'head'), axis=0, tiled=True)  54.7 us
    all_to_all x1, blocking collectives, per_device(): lax.all_to_all(result, 'seq', split_axis=2, concat_axis=3, tiled=True)  53.2 us
    all_gather x1, waiting for transfers between devices, per_device(): lax.all_gather(values, ('span', 'head'), axis=0, tiled=True)  48.2 us
    dot_general x4, matrix products, advance(): jnp.einsum('hqk,khd->hqd', weights, value_block, preferred_element_type=j...  46.2 us
    unnamed x10, local copies, waits for them, and re-layouts  14.9 us
    unnamed x4, other arithmetic  13 us
  transfers between devices with their start and end apart: 2, of which 2 were waited for; matrix products, arithmetic and copies ran while one was open for 4% of the time, Pallas kernels for 0%

commit v1 on v0

--- a/solution.py
+++ b/solution.py
@@ -100,7 +100,10 @@
         bias_rate,
     )
     result = finish(running)
-    return lax.all_to_all(result, "seq", split_axis=2, concat_axis=3, tiled=True)
+    return jnp.concatenate(
+        lax.all_to_all(jnp.stack(jnp.split(result, lax.axis_size("seq"), axis=2)), "seq", 0, 0),
+        axis=3,
+    )
 
 
 def solution(mesh):

time: 447 us -> 413 us (0.924)
  local copies, waits for them, and re-layouts: 57.9 us -> 36.9 us
  other arithmetic: 104 us -> 91.4 us
    unnamed x4 -> x3, other arithmetic: 13 us -> 0.01 us
    unnamed x10 -> x6, local copies, waits for them, and re-layouts: 14.9 us -> 5.25 us
    convert_element_type x1 -> x0, local copies, waits for them, and re-layouts: 7.75 us -> none  [finish(): output.reshape(1, 1, query_count, local_heads * HD).astype(jnp.bfloat16)]
    all_to_all x2 -> x0, local copies, waits for them, and re-layouts: 6.68 us -> none  [per_device(): lax.all_to_all(result, 'seq', split_axis=2, concat_axis=3, tiled=True)]
  transfers between devices with their start and end apart: 2 -> 2, of which waited for: 2 -> 2; matrix products, arithmetic and copies ran while one was open for 4% -> 5% of each run, Pallas kernels for 0% -> 0%
where the time goes in v1:
time: 413 us; the launch traced here: 412 us
  matrix products  112 us (27%)
  waiting for transfers between devices  104 us (25%)
  other arithmetic  91.4 us (22%)
  blocking collectives  53 us (13%)
  local copies, waits for them, and re-layouts  36.9 us (9%)
  between operations  13.5 us (3%)
    reduce_sum x4, other arithmetic, advance(): totals = totals * shrink + jnp.sum(weights.astype(jnp.float32), axis=2)  86.4 us
    dot_general x4, matrix products, advance(): jnp.einsum('qhd,khd->hqk', query_heads, key_block, preferred_element_type...  66.3 us
    all_gather x1, waiting for transfers between devices, per_device(): lax.all_gather(keys, ('span', 'head'), axis=0, tiled=True)  54.7 us
    all_to_all x1, blocking collectives, per_device(): lax.all_to_all(jnp.stack(jnp.split(result, lax.axis_size('seq'), axis=2))...  53 us
    all_gather x1, waiting for transfers between devices, per_device(): lax.all_gather(values, ('span', 'head'), axis=0, tiled=True)  48.2 us
    dot_general x4, matrix products, advance(): jnp.einsum('hqk,khd->hqd', weights, value_block, preferred_element_type=j...  46.2 us
    all_gather x1, local copies, waits for them, and re-layouts, per_device(): lax.all_gather(keys, ('span', 'head'), axis=0, tiled=True)  11.6 us
    all_gather x1, local copies, waits for them, and re-layouts, per_device(): lax.all_gather(values, ('span', 'head'), axis=0, tiled=True)  11.4 us
  transfers between devices with their start and end apart: 2, of which 2 were waited for; matrix products, arithmetic and copies ran while one was open for 5% of the time, Pallas kernels for 0%

profile of v1, /device:TPU:0, one launch (start us, length us, event | category | flops | bytes accessed | tf_op | source)
XLA Modules:
  0.0 411.7 jit_solution(17819397767490333471)
XLA Ops:
  6.5 0.7 all-gather.3.cloned.1.call-update
  8.1 2.9 copy.33
  10.9 2.4 copy.36
  15.2 54.7 %all-gather.3.cloned.1.call-done = bf16[4,1,1024,1024]{3,2,1,0:T(8,128)(2,1)} async-done(((bf16[1,1,1024,1024]{3,2,1,0:T(8,128)(2,1)}), bf16[4,1,1024,1024]{3,2,1,0:T(8,128)(2,1)}) %all-gather.3.cloned.1.call-update) | async-done | bytes 8388624 | tf_op jit(solution)/shard_map/all_gather | solution.py:86
  69.9 11.6 %copy.32 = bf16[4,1,1024,1024]{2,3,0,1:T(8,128)(2,1)} copy(bf16[4,1,1024,1024]{3,2,1,0:T(8,128)(2,1)} %all-gather.3.cloned.1.call-done) | data formatting | bytes 16777216 | tf_op jit(solution)/shard_map/all_gather | solution.py:86
  81.5 48.2 %all-gather.5.cloned.1.call-done = bf16[4,1,1024,1024]{3,2,1,0:T(8,128)(2,1)} async-done(((bf16[1,1,1024,1024]{3,2,1,0:T(8,128)(2,1)}), bf16[4,1,1024,1024]{3,2,1,0:T(8,128)(2,1)}) %all-gather.5.cloned.1.call-update) | async-done | bytes 8388624 | tf_op jit(solution)/shard_map/all_gather | solution.py:87
  129.8 11.4 %copy.34 = bf16[4,1,1024,1024]{2,3,0,1:T(8,128)(2,1)} copy(bf16[4,1,1024,1024]{3,2,1,0:T(8,128)(2,1)} %all-gather.5.cloned.1.call-done) | data formatting | bytes 16777216 | tf_op jit(solution)/shard_map/all_gather | solution.py:87
  141.3 199.1 %while.15 = (s32[]{:T(128)}, f32[8,1024]{1,0:T(8,128)S(1)}, f32[8,1024]{1,0:T(8,128)S(1)}, f32[8,1024,128]{2,1,0:T(8,128)}, pred[4,1024]{1,0:T(4,128)(4,1)S(1)},...) while((s32[]{:T(128)}, f32[8,1024]{1,0:T(8,128)S(1)}, ...), condition=%wide.region_5.6_spmd.clone, body=%wide.region_2.5_spmd.clone.sunk | while | flops 4398817280 | bytes 115856512 | solution.py:63
  141.3 16.6 %bitcast_reduce_fusion.2 = (f32[8,1024]{1,0:T(8,128)S(1)}, f32[8,1024,1024]{2,1,0:T(8,128)}) fusion(f32[1024]{0:T(1024)S(1)} %bitcast.59, pred[1024]{0:T(1024)(128)(4,1)S(1)} %dynamic-slice_reduce_fusion.2, bf16[1024,8,128]{2,0,1:T(8,128)(2,1)S(1)} %get-tuple-element.235, bf16[4,1024,8,128]{1,3,2,0:T(8,128)(2,1)} %get-tuple-element.234, ...), kind=kOutput, calls=%fused_computation.1.clone.1 | convolution fusion | flops 2181029888 | bytes 37787136 | tf_op jit(solution)/shard_map/while/body/eval_jaxpr/qhd,khd->hqk/dot_general | solution.py:47
  157.9 21.6 %convert_reduce_fusion.2 = (f32[8,1024]{1,0:T(8,128)S(1)}, bf16[8,1024,1024]{1,2,0:T(8,128)(2,1)}) fusion(f32[8,1024]{1,0:T(8,128)S(1)} %select_maximum_fusion.2, f32[1024]{0:T(1024)S(1)} %bitcast.60, f32[8,1024,1024]{2,1,0:T(8,128)} %get-tuple-element.202, pred[1024]{0:T(1024)(128)(4,1)S(1)} %dynamic-slice_reduce_fusion.2), kind=kLoop, calls=%fused_computation.5.clone.1 | loop fusion | flops 67100672 | bytes 50402304 | tf_op jit(solution)/shard_map/while/body/eval_jaxpr/reduce_sum | solution.py:57
  179.5 11.0 %fusion.29 = f32[8,1024,128]{2,1,0:T(8,128)} fusion(f32[8,1024,128]{2,1,0:T(8,128)} %get-tuple-element.221, f32[8,1024]{1,0:T(8,128)S(1)} %get-tuple-element.205, pred[]{:T(512)S(6)} %compare.7, bf16[8,1024,1024]{1,2,0:T(8,128)(2,1)} %get-tuple-element.206, bf16[4,1024,8,128]{1,3,2,0:T(8,128)(2,1)} %get-tuple-element.237, s32[]{:T(128)} %get-tuple-element.218), kind=kOutput, calls=%fused_computation.8.clone.1 | convolution fusion | flops 2150629376 | bytes 27296256 | tf_op jit(solution)/shard_map/while/body/eval_jaxpr/hqk,khd->hqd/dot_general | solution.py:58
  190.5 16.6 %bitcast_reduce_fusion.2 = (f32[8,1024]{1,0:T(8,128)S(1)}, f32[8,1024,1024]{2,1,0:T(8,128)}) fusion(f32[1024]{0:T(1024)S(1)} %bitcast.59, pred[1024]{0:T(1024)(128)(4,1)S(1)} %dynamic-slice_reduce_fusion.2, bf16[1024,8,128]{2,0,1:T(8,128)(2,1)S(1)} %get-tuple-element.235, bf16[4,1024,8,128]{1,3,2,0:T(8,128)(2,1)} %get-tuple-element.234, ...), kind=kOutput, calls=%fused_computation.1.clone.1 | convolution fusion | flops 2181029888 | bytes 37787136 | tf_op jit(solution)/shard_map/while/body/eval_jaxpr/qhd,khd->hqk/dot_general | solution.py:47
  207.1 21.6 %convert_reduce_fusion.2 = (f32[8,1024]{1,0:T(8,128)S(1)}, bf16[8,1024,1024]{1,2,0:T(8,128)(2,1)}) fusion(f32[8,1024]{1,0:T(8,128)S(1)} %select_maximum_fusion.2, f32[1024]{0:T(1024)S(1)} %bitcast.60, f32[8,1024,1024]{2,1,0:T(8,128)} %get-tuple-element.202, pred[1024]{0:T(1024)(128)(4,1)S(1)} %dynamic-slice_reduce_fusion.2), kind=kLoop, calls=%fused_computation.5.clone.1 | loop fusion | flops 67100672 | bytes 50402304 | tf_op jit(solution)/shard_map/while/body/eval_jaxpr/reduce_sum | solution.py:57
  228.7 11.7 %fusion.29 = f32[8,1024,128]{2,1,0:T(8,128)} fusion(f32[8,1024,128]{2,1,0:T(8,128)} %get-tuple-element.221, f32[8,1024]{1,0:T(8,128)S(1)} %get-tuple-element.205, pred[]{:T(512)S(6)} %compare.7, bf16[8,1024,1024]{1,2,0:T(8,128)(2,1)} %get-tuple-element.206, bf16[4,1024,8,128]{1,3,2,0:T(8,128)(2,1)} %get-tuple-element.237, s32[]{:T(128)} %get-tuple-element.218), kind=kOutput, calls=%fused_computation.8.clone.1 | convolution fusion | flops 2150629376 | bytes 27296256 | tf_op jit(solution)/shard_map/while/body/eval_jaxpr/hqk,khd->hqd/dot_general | solution.py:58
  240.5 16.6 %bitcast_reduce_fusion.2 = (f32[8,1024]{1,0:T(8,128)S(1)}, f32[8,1024,1024]{2,1,0:T(8,128)}) fusion(f32[1024]{0:T(1024)S(1)} %bitcast.59, pred[1024]{0:T(1024)(128)(4,1)S(1)} %dynamic-slice_reduce_fusion.2, bf16[1024,8,128]{2,0,1:T(8,128)(2,1)S(1)} %get-tuple-element.235, bf16[4,1024,8,128]{1,3,2,0:T(8,128)(2,1)} %get-tuple-element.234, ...), kind=kOutput, calls=%fused_computation.1.clone.1 | convolution fusion | flops 2181029888 | bytes 37787136 | tf_op jit(solution)/shard_map/while/body/eval_jaxpr/qhd,khd->hqk/dot_general | solution.py:47
  257.1 21.6 %convert_reduce_fusion.2 = (f32[8,1024]{1,0:T(8,128)S(1)}, bf16[8,1024,1024]{1,2,0:T(8,128)(2,1)}) fusion(f32[8,1024]{1,0:T(8,128)S(1)} %select_maximum_fusion.2, f32[1024]{0:T(1024)S(1)} %bitcast.60, f32[8,1024,1024]{2,1,0:T(8,128)} %get-tuple-element.202, pred[1024]{0:T(1024)(128)(4,1)S(1)} %dynamic-slice_reduce_fusion.2), kind=kLoop, calls=%fused_computation.5.clone.1 | loop fusion | flops 67100672 | bytes 50402304 | tf_op jit(solution)/shard_map/while/body/eval_jaxpr/reduce_sum | solution.py:57
  278.7 11.7 %fusion.29 = f32[8,1024,128]{2,1,0:T(8,128)} fusion(f32[8,1024,128]{2,1,0:T(8,128)} %get-tuple-element.221, f32[8,1024]{1,0:T(8,128)S(1)} %get-tuple-element.205, pred[]{:T(512)S(6)} %compare.7, bf16[8,1024,1024]{1,2,0:T(8,128)(2,1)} %get-tuple-element.206, bf16[4,1024,8,128]{1,3,2,0:T(8,128)(2,1)} %get-tuple-element.237, s32[]{:T(128)} %get-tuple-element.218), kind=kOutput, calls=%fused_computation.8.clone.1 | convolution fusion | flops 2150629376 | bytes 27296256 | tf_op jit(solution)/shard_map/while/body/eval_jaxpr/hqk,khd->hqd/dot_general | solution.py:58
  290.5 16.6 %bitcast_reduce_fusion.2 = (f32[8,1024]{1,0:T(8,128)S(1)}, f32[8,1024,1024]{2,1,0:T(8,128)}) fusion(f32[1024]{0:T(1024)S(1)} %bitcast.59, pred[1024]{0:T(1024)(128)(4,1)S(1)} %dynamic-slice_reduce_fusion.2, bf16[1024,8,128]{2,0,1:T(8,128)(2,1)S(1)} %get-tuple-element.235, bf16[4,1024,8,128]{1,3,2,0:T(8,128)(2,1)} %get-tuple-element.234, ...), kind=kOutput, calls=%fused_computation.1.clone.1 | convolution fusion | flops 2181029888 | bytes 37787136 | tf_op jit(solution)/shard_map/while/body/eval_jaxpr/qhd,khd->hqk/dot_general | solution.py:47
  307.1 21.6 %convert_reduce_fusion.2 = (f32[8,1024]{1,0:T(8,128)S(1)}, bf16[8,1024,1024]{1,2,0:T(8,128)(2,1)}) fusion(f32[8,1024]{1,0:T(8,128)S(1)} %select_maximum_fusion.2, f32[1024]{0:T(1024)S(1)} %bitcast.60, f32[8,1024,1024]{2,1,0:T(8,128)} %get-tuple-element.202, pred[1024]{0:T(1024)(128)(4,1)S(1)} %dynamic-slice_reduce_fusion.2), kind=kLoop, calls=%fused_computation.5.clone.1 | loop fusion | flops 67100672 | bytes 50402304 | tf_op jit(solution)/shard_map/while/body/eval_jaxpr/reduce_sum | solution.py:57
  328.7 11.7 %fusion.29 = f32[8,1024,128]{2,1,0:T(8,128)} fusion(f32[8,1024,128]{2,1,0:T(8,128)} %get-tuple-element.221, f32[8,1024]{1,0:T(8,128)S(1)} %get-tuple-element.205, pred[]{:T(512)S(6)} %compare.7, bf16[8,1024,1024]{1,2,0:T(8,128)(2,1)} %get-tuple-element.206, bf16[4,1024,8,128]{1,3,2,0:T(8,128)(2,1)} %get-tuple-element.237, s32[]{:T(128)} %get-tuple-element.218), kind=kOutput, calls=%fused_computation.8.clone.1 | convolution fusion | flops 2150629376 | bytes 27296256 | tf_op jit(solution)/shard_map/while/body/eval_jaxpr/hqk,khd->hqd/dot_general | solution.py:58
  340.4 5.4 %copy.38 = f32[8,1024,128]{1,2,0:T(8,128)} copy(f32[8,1024,128]{2,1,0:T(8,128)} %get-tuple-element.53) | data formatting | bytes 8388608 | tf_op jit(solution)/shard_map/while | solution.py:63
  345.8 2.8 divide_convert_fusion
  349.0 53.0 %all_to_all.5 = bf16[4,1,1,256,1024]{3,4,2,1,0:T(8,128)(2,1)S(1)} all-to-all(bf16[4,1,1,256,1024]{3,4,2,1,0:T(8,128)(2,1)S(1)} %pad_maximum_fusion), channel_id=1, replica_groups=mesh['rep'=2,'span'=2,'seq'=4,'head'=2] {'seq'}, dimensions={0} | all-to-all | bytes 4194304 | tf_op jit(solution)/shard_map/all_to_all | solution.py:104
  402.0 2.8 copy.41
  (39 shorter events, 3.4 us)
Async XLA Ops:
  6.5 63.4 %all-gather.3.cloned.1.call-start = ((), (), s32[]{:S(2)}) async-start(), calls=%async_computation.1 | async-start | bytes 10485760 | tf_op jit(solution)/shard_map/all_gather | solution.py:86
  7.3 122.5 %all-gather.5.cloned.1.call-start = ((), (), s32[]{:S(2)}) async-start(), calls=%async_computation.2 | async-start | bytes 10485760 | tf_op jit(solution)/shard_map/all_gather | solution.py:87
  8.0 5.3 %copy-start.1 = (s32[2]{0:T(128)S(1)}, s32[2]{0:T(128)}, u32[]{:S(2)}) copy-start(s32[2]{0:T(128)} %param.9) | copy-start | bytes 28
  81.5 59.7 %copy-start = (bf16[1024,8,128]{2,0,1:T(8,128)(2,1)S(1)}, bf16[1024,8,128]{2,0,1:T(8,128)(2,1)}, u32[]{:S(2)}) copy-start(bf16[1024,8,128]{2,0,1:T(8,128)(2,1)} %copy.36) | copy-start | bytes 6291460
Sparse Core Ops, SparseCore 0:
  8.9 60.9 all-gather.2
  71.5 58.2 all-gather.4
